TPU v7x, 256 devices: a whole 4x4x8 slice. The times are simulated.
256 devices in a mesh: grp: 16 (over z, y_lo), blk: 16 (over y_hi, x, core).
Axes of the slice: x: 4, y: 4 (y_hi: 2, y_lo: 2; y = y_hi * 2 + y_lo), z: 8, core: 2. Of those that a mesh axis runs over, the one named last changes fastest.
Arguments:
- states: bfloat16 [524288, 768], P(('grp', 'blk')), may hold values from -6 to 6
- query_weight: bfloat16 [768, 768], replicated, may hold values from -0.21875 to 0.21875
- attempts: bfloat16 [16384, 768], P(('grp', 'blk')), may hold values from -6 to 6
- attempt_theorem: int32 [16384], P('grp'), may hold values from 0 to 15
- positive: int32 [524288], P(('grp', 'blk')), may hold values from 0 to 1023
Outputs:
- loss: float32 [524288], P(('grp', 'blk'))
- grad_attempts: float32 [16384, 768], P(('grp', 'blk'))
- grad_weight: float32 [768, 768], replicated
All inputs are finite; a program needn't handle non-finite values.
Results may differ from a plain program's by a relative error of at most 0.012.
Values may be sent and summed in bfloat16 or wider, within the bound.
No kernel may reach another device: no remote copies, remote signals or barrier semaphores. Data moves between devices by JAX's collectives and lax.ppermute only.
A program may use at most 64 MiB of HBM per device.

v0:
```python
import jax
import jax.numpy as jnp
from jax import lax
from jax.sharding import PartitionSpec as P

logit_sharpness = 0.07
epsilon = 1e-06


def normalized_rows(values):
    return values * lax.rsqrt(jnp.mean(values * values, axis=-1, keepdims=True) + epsilon)


def on_device(states, query_weight, attempts, attempt_theorem, positive):
    vector_dimension = states.shape[1]
    logit_multiplier = 1.0 / (logit_sharpness * vector_dimension)
    attempt_rows_float, attempt_back = jax.vjp(normalized_rows, attempts.astype(jnp.float32))
    candidate_direction = attempt_rows_float.astype(jnp.bfloat16)
    proj = jnp.dot(states, query_weight, preferred_element_type=jnp.float32)
    query_float, query_back = jax.vjp(normalized_rows, proj)
    query_unit = query_float.astype(jnp.bfloat16)
    anchor_lemma_label = jnp.take(attempt_theorem, positive)
    panel = lax.all_gather(candidate_direction, "blk", axis=0, tiled=True)
    scores = (
        lax.dot_general(
            query_unit, panel, (((1,), (1,)), ((), ())), preferred_element_type=jnp.float32
        )
        * logit_multiplier
    )
    mask = anchor_lemma_label[:, None] == attempt_theorem[None, :]
    expo = jnp.where(mask, jnp.exp(scores), 0.0)
    total = jnp.sum(expo, axis=1)
    columns = lax.broadcasted_iota(jnp.int32, scores.shape, 1)
    chosen = columns == positive[:, None]
    pos_score = jnp.sum(jnp.where(chosen, scores, 0.0), axis=1)
    losses = jnp.log(total) - pos_score
    weights = (expo / total[:, None] - chosen.astype(jnp.float32)).astype(jnp.bfloat16)
    grad_qunit = jnp.dot(weights, panel, preferred_element_type=jnp.float32) * logit_multiplier
    grad_aunit = lax.psum_scatter(
        (
            lax.dot_general(
                weights, query_unit, (((0,), (0,)), ((), ())), preferred_element_type=jnp.float32
            )
            * logit_multiplier
        ).astype(jnp.bfloat16),
        "blk",
        scatter_dimension=0,
        tiled=True,
    ).astype(jnp.float32)
    grad_attempts = attempt_back(grad_aunit)[0]
    grad_proj = query_back(grad_qunit)[0].astype(jnp.bfloat16)
    weight_term = lax.dot_general(
        states, grad_proj, (((0,), (0,)), ((), ())), preferred_element_type=jnp.float32
    )
    grad_weight = lax.psum(weight_term, ("grp", "blk"))
    return (losses, grad_attempts, grad_weight)


def solution(mesh):
    in_specs = (P(("grp", "blk"), None), P(), P(("grp", "blk"), None), P("grp"), P(("grp", "blk")))
    out_specs = (P(("grp", "blk")), P(("grp", "blk"), None), P())
    return jax.shard_map(
        on_device, mesh=mesh, in_specs=in_specs, out_specs=out_specs, check_vma=False
    )
```

profile of v0, /device:TPU:2, one launch (start us, length us, event | category | flops | bytes accessed | tf_op | source)
XLA Modules:
  0.0 437.2 jit_solution(6341290176718321154)
XLA Ops:
  7.2 0.0 copy-start
  7.2 0.0 all-gather.2.cloned.1.call-start
  7.2 1.2 fusion.10
  8.4 1.6 fusion.11
  10.0 0.0 all-gather.2.cloned.1.call-update
  10.1 0.0 all-reduce.2.cloned.1.call-start
  10.1 0.7 fusion.14
  10.8 10.2 %gather_fusion = s32[2048]{0:T(1024)S(1)} fusion(s32[1024]{0:T(1024)} %param.8, s32[2048]{0:T(1024)S(1)} %fusion.14), kind=kCustom, calls=%fused_computation | custom fusion | bytes 24576 | tf_op jit(solution)/shard_map/jit(_take)/gather | solution.py:22
  21.1 0.0 copy-start.4
  21.1 0.0 copy-start.1
  21.1 5.8 %multiply_reduce_fusion.1 = (f32[2048]{0:T(1024)S(1)}, f32[2048,768]{0,1:T(8,128)}) fusion(bf16[2048,768]{1,0:T(8,128)(2,1)S(1)} %copy-done, bf16[768,768]{1,0:T(8,128)(2,1)} %param.6), kind=kOutput, calls=%fused_computation.10 | convolution fusion | flops 2419062784 | bytes 10625024 | tf_op jit(solution)/shard_map/dot_general | solution.py:19
  26.9 38.6 %all-gather.2.cloned.1.call-done = bf16[1024,768]{1,0:T(8,128)(2,1)} async-done(((bf16[64,768]{1,0:T(8,128)(2,1)}), bf16[1024,768]{1,0:T(8,128)(2,1)}) %all-gather.2.cloned.1.call-update) | async-done | bytes 1572880 | tf_op jit(solution)/shard_map/all_gather | solution.py:23
  65.5 8.2 %fusion = (f32[2048]{0:T(1024)S(1)}, f32[2048]{0:T(1024)S(1)}, f32[2048,1024]{0,1:T(8,128)S(1)}) fusion(s32[2048]{0:T(1024)S(1)} %and_select_fusion, s32[1024]{0:T(1024)S(1)} %copy-done.1, s32[2048]{0:T(1024)S(1)} %copy-done.4, bf16[1024,768]{1,0:T(8,128)(2,1)} %all-gather.2.cloned.1.call-done, f32[2048,768]{0,1:T(8,128)} %get-tuple-element.14, ...), kind=kOutput, calls=%fused_computation.6 | convolution fusion | flops 3239047168 | bytes 16297984 | tf_op jit(solution)/shard_map/dot_general | solution.py:25
  73.7 0.0 copy-start.5
  73.7 0.0 copy-start.6
  73.7 3.8 subtract_convert_fusion
  77.6 0.0 copy-done.5
  77.6 0.0 copy-done.6
  77.6 0.0 copy-start.2
  77.6 4.1 multiply_reduce_fusion
  81.7 4.5 %fusion.6 = f32[768,768]{0,1:T(8,128)} fusion(bf16[2048,768]{1,0:T(8,128)(2,1)S(1)} %copy-done, f32[2048,768]{0,1:T(8,128)S(1)} %copy-done.6, f32[2048,768]{0,1:T(8,128)S(1)} %get-tuple-element.17, f32[2048]{0:T(1024)S(1)} %get-tuple-element.12, f32[2048]{0:T(1024)S(1)} %get-tuple-element.11), kind=kOutput, calls=%fused_computation.15 | convolution fusion | flops 2423783424 | bytes 18104320 | tf_op jit(solution)/shard_map/dot_general | solution.py:52
  86.2 0.0 all-reduce.2.cloned.1.call-update
  86.2 0.0 reduce-scatter.2.cloned.1.call-start
  86.2 8.7 %multiply_convert_fusion.1 = bf16[1024,768]{1,0:T(8,128)(2,1)} fusion(bf16[2048,1024]{0,1:T(8,128)(2,1)} %copy-done.2, f32[2048,768]{0,1:T(8,128)} %get-tuple-element.14, f32[2048]{0:T(1024)S(1)} %fusion.13), kind=kOutput, calls=%fused_computation.14 | convolution fusion | flops 3225944064 | bytes 12066816 | tf_op jit(solution)/shard_map/dot_general | solution.py:41
  94.9 0.0 reduce-scatter.2.cloned.1.call-update
  95.0 0.6 log_subtract_fusion
  95.6 253.1 %all-reduce.2.cloned.1.call-done = f32[768,768]{0,1:T(8,128)} async-done(((f32[768,768]{0,1:T(8,128)}), f32[768,768]{0,1:T(8,128)}) %all-reduce.2.cloned.1.call-update) | async-done | bytes 2359312 | tf_op jit(solution)/shard_map/psum | solution.py:55
  348.7 3.0 copy.9
  351.7 76.2 %reduce-scatter.2.cloned.1.call-done = bf16[64,768]{1,0:T(8,128)(2,1)} async-done(((bf16[1024,768]{1,0:T(8,128)(2,1)}), bf16[64,768]{1,0:T(8,128)(2,1)}) %reduce-scatter.2.cloned.1.call-update) | async-done | bytes 98320 | tf_op jit(solution)/shard_map/reduce_scatter | solution.py:39
  427.9 0.0 copy-done.3
  427.9 1.0 fusion.12
  428.9 1.7 add_add_fusion.1
  (10 shorter events, 0.1 us)
Async XLA Ops:
  7.2 13.9 %copy-start = (bf16[2048,768]{1,0:T(8,128)(2,1)S(1)}, bf16[2048,768]{1,0:T(8,128)(2,1)}, u32[]{:S(2)}) copy-start(bf16[2048,768]{1,0:T(8,128)(2,1)} %param.5) | copy-start | bytes 9437188
  7.2 58.3 %all-gather.2.cloned.1.call-start = ((), (), s32[]{:S(2)}) async-start(), calls=%async_computation.1 | async-start | bytes 1671168 | tf_op jit(solution)/shard_map/all_gather | solution.py:23
  10.1 338.6 %all-reduce.2.cloned.1.call-start = ((), (), s32[]{:S(2)}) async-start(), calls=%async_computation.3 | async-start | bytes 4718592 | tf_op jit(solution)/shard_map/psum | solution.py:55
  21.1 5.9 %copy-start.4 = (s32[2048]{0:T(1024)S(1)}, s32[2048]{0:T(1024)}, u32[]{:S(2)}) copy-start(s32[2048]{0:T(1024)} %param.9) | copy-start | bytes 24580
  21.1 44.5 %copy-start.1 = (s32[1024]{0:T(1024)S(1)}, s32[1024]{0:T(1024)}, u32[]{:S(2)}) copy-start(s32[1024]{0:T(1024)} %param.8) | copy-start | bytes 12292
  73.7 3.9 copy-start.5
  73.7 3.9 copy-start.6
  77.6 4.1 copy-start.2
  86.2 341.7 %reduce-scatter.2.cloned.1.call-start = ((), (), s32[]{:S(2)}) async-start(), calls=%async_computation.2 | async-start | bytes 1671168 | tf_op jit(solution)/shard_map/reduce_scatter | solution.py:39
  94.9 333.0 %copy-start.3 = (bf16[64,768]{1,0:T(8,128)(2,1)S(1)}, bf16[64,768]{1,0:T(8,128)(2,1)}, u32[]{:S(2)}) copy-start(bf16[64,768]{1,0:T(8,128)(2,1)} %param.7) | copy-start | bytes 294916
Sparse Core Ops, SparseCore 0:
  11.3 54.1 all-gather.1
  86.3 262.3 all-reduce.1
  352.8 75.0 reduce-scatter.1
where the time goes:
time: 437 us
  waiting for transfers between devices  368 us (84%)
  matrix products  31.2 us (7%)
  between operations  13.9 us (3%)
  local copies, waits for them, and re-layouts  13.3 us (3%)
  other arithmetic  10.7 us (2%)
    psum x1, waiting for transfers between devices, on_device(): grad_weight = lax.psum(weight_term, ('grp', 'blk'))  253 us
    reduce_scatter x1, waiting for transfers between devices, on_device(): lax.psum_scatter((lax.dot_general(weights, query_unit, (((0,), (0,)), (()...  76.2 us
    all_gather x1, waiting for transfers between devices, on_device(): panel = lax.all_gather(candidate_direction, 'blk', axis=0, tiled=True)  38.6 us
    gather x1, local copies, waits for them, and re-layouts, on_device(): anchor_lemma_label = jnp.take(attempt_theorem, positive)  10.2 us
  transfers between devices with their start and end apart: 3, of which 3 were waited for; matrix products, arithmetic and copies ran while one was open for 7% of the time, Pallas kernels for 0%

commit v1 on v0

--- a/solution.py
+++ b/solution.py
@@ -20,7 +20,15 @@
     query_float, query_back = jax.vjp(normalized_rows, proj)
     query_unit = query_float.astype(jnp.bfloat16)
     anchor_lemma_label = jnp.take(attempt_theorem, positive)
-    panel = lax.all_gather(candidate_direction, "blk", axis=0, tiled=True)
+    panel = jnp.concatenate(
+        jax.lax.all_to_all(
+            jnp.stack([candidate_direction for _ in range(jax.lax.axis_size("blk"))], axis=0),
+            "blk",
+            0,
+            0,
+        ),
+        axis=0,
+    )
     scores = (
         lax.dot_general(
             query_unit, panel, (((1,), (1,)), ((), ())), preferred_element_type=jnp.float32

time: 437 us -> 341 us (0.78)
  waiting for transfers between devices: 368 us -> 261 us
  starting transfers between devices: 0.12 us -> 7.56 us
    reduce_scatter x1, waiting for transfers between devices: 76.2 us -> 0.01 us  [on_device(): lax.psum_scatter((lax.dot_general(weights, query_unit, (((0,), (0,)), (()...]
    all_gather x1 -> x0, waiting for transfers between devices: 38.6 us -> none  [on_device(): panel = lax.all_gather(candidate_direction, 'blk', axis=0, tiled=True)]
    all_to_all x0 -> x1, starting transfers between devices: none -> 7.48 us  [on_device(): jax.lax.all_to_all(jnp.stack([candidate_direction for _ in range(jax.lax....]
    all_to_all x0 -> x1, waiting for transfers between devices: none -> 6.08 us  [on_device(): jax.lax.all_to_all(jnp.stack([candidate_direction for _ in range(jax.lax....]
  transfers between devices with their start and end apart: 3 -> 3, of which waited for: 3 -> 2; matrix products, arithmetic and copies ran while one was open for 7% -> 8% of each run, Pallas kernels for 0% -> 0%
where the time goes in v1:
time: 341 us
  waiting for transfers between devices  261 us (77%)
  matrix products  33.8 us (10%)
  between operations  15.6 us (5%)
  local copies, waits for them, and re-layouts  13 us (4%)
  other arithmetic  10.1 us (3%)
  starting transfers between devices  7.56 us (2%)
    psum x1, waiting for transfers between devices, on_device(): grad_weight = lax.psum(weight_term, ('grp', 'blk'))  255 us
    dot_general x1, matrix products, on_device(): lax.dot_general(weights, query_unit, (((0,), (0,)), ((), ())), preferred_...  8.7 us
    gather x1, local copies, waits for them, and re-layouts, on_device(): anchor_lemma_label = jnp.take(attempt_theorem, positive)  8.58 us
    dot_general x1, matrix products, on_device(): lax.dot_general(query_unit, panel, (((1,), (1,)), ((), ())), preferred_el...  8.19 us
    all_to_all x1, starting transfers between devices, on_device(): jax.lax.all_to_all(jnp.stack([candidate_direction for _ in range(jax.lax....  7.48 us
  transfers between devices with their start and end apart: 3, of which 2 were waited for; matrix products, arithmetic and copies ran while one was open for 8% of the time, Pallas kernels for 0%

profile of v1, /device:TPU:2, one launch (start us, length us, event | category | flops | bytes accessed | tf_op | source)
XLA Modules:
  0.0 341.0 jit_solution(2533566730686601054)
XLA Ops:
  8.0 0.0 copy-start
  8.0 0.0 copy-start.1
  8.0 1.2 fusion.10
  9.2 1.0 fusion.11
  10.2 1.3 stack.2
  11.5 7.5 %all-to-all-start = ((bf16[16,64,768]{2,1,0:T(8,128)(2,1)}), bf16[16,64,768]{2,1,0:T(8,128)(2,1)}, u32[]{:S(2)}, u32[]{:S(2)}) async-start(bf16[16,64,768]{2,1,0:T(8,128)(2,1)} %stack.2), calls=%async_computation | async-start | bytes 3145728 | tf_op jit(solution)/shard_map/all_to_all | solution.py:24
  19.0 0.0 all-reduce.2.cloned.1.call-start
  19.0 0.7 fusion.14
  19.7 0.0 copy-done.1
  19.7 8.6 %gather_fusion = s32[2048]{0:T(1024)S(1)} fusion(s32[1024]{0:T(1024)S(1)} %copy-done.1, s32[2048]{0:T(1024)S(1)} %fusion.14), kind=kCustom, calls=%fused_computation | custom fusion | bytes 24576 | tf_op jit(solution)/shard_map/jit(_take)/gather | solution.py:22
  28.3 0.0 copy-done
  28.3 0.0 copy-start.4
  28.3 5.8 %multiply_reduce_fusion.1 = (f32[2048]{0:T(1024)S(1)}, f32[2048,768]{0,1:T(8,128)}) fusion(bf16[2048,768]{1,0:T(8,128)(2,1)S(1)} %copy-done, bf16[768,768]{1,0:T(8,128)(2,1)} %param.6), kind=kOutput, calls=%fused_computation.10 | convolution fusion | flops 2419062784 | bytes 10625024 | tf_op jit(solution)/shard_map/dot_general | solution.py:19
  34.2 0.0 copy-done.4
  34.2 6.1 %all-to-all-done = bf16[16,64,768]{2,1,0:T(8,128)(2,1)} async-done(((bf16[16,64,768]{2,1,0:T(8,128)(2,1)}), bf16[16,64,768]{2,1,0:T(8,128)(2,1)}, u32[]{:S(2)}, u32[]{:S(2)}) %all-to-all-start) | async-done | bytes 1572896 | tf_op jit(solution)/shard_map/all_to_all | solution.py:24
  40.3 8.2 %fusion = (f32[2048]{0:T(1024)S(1)}, f32[2048]{0:T(1024)S(1)}, f32[2048,1024]{0,1:T(8,128)S(1)}) fusion(s32[2048]{0:T(1024)S(1)} %and_select_fusion, s32[1024]{0:T(1024)S(1)} %copy-done.1, s32[2048]{0:T(1024)S(1)} %copy-done.4, bf16[1024,768]{1,0:T(8,128)(2,1)} %bitcast, f32[2048,768]{0,1:T(8,128)} %get-tuple-element.14, f32[2048]{0:T(1024)S(1)} %fusion.13), kind=kOutput, calls=%fused_computation.6 | convolution fusion | flops 3239047168 | bytes 16297984 | tf_op jit(solution)/shard_map/dot_general | solution.py:33
  48.5 0.0 copy-start.5
  48.5 3.8 %subtract_convert_fusion = bf16[2048,1024]{0,1:T(8,128)(2,1)S(1)} fusion(f32[2048,1024]{0,1:T(8,128)S(1)} %get-tuple-element.15, f32[2048]{0:T(1024)S(1)} %get-tuple-element.9, s32[2048]{0:T(1024)S(1)} %copy-done.4, s32[2048]{0:T(1024)S(1)} %and_select_fusion, s32[1024]{0:T(1024)S(1)} %copy-done.1), kind=kLoop, calls=%fused_computation.2 | loop fusion | flops 16777216 | bytes 12611584 | tf_op jit(solution)/shard_map/convert_element_type | solution.py:45
  52.3 0.0 copy-done.5
  52.3 0.0 copy-start.2
  52.3 6.6 %multiply_reduce_fusion = (f32[2048]{0:T(1024)S(1)}, f32[2048,768]{0,1:T(8,128)S(1)}) fusion(f32[2048,768]{0,1:T(8,128)S(1)} %copy-done.5, bf16[2048,1024]{0,1:T(8,128)(2,1)S(1)} %subtract_convert_fusion, bf16[1024,768]{1,0:T(8,128)(2,1)} %bitcast), kind=kOutput, calls=%fused_computation.8 | convolution fusion | flops 3225942016 | bytes 18358272 | tf_op jit(solution)/shard_map/dot_general | solution.py:46
  59.0 4.5 %fusion.6 = f32[768,768]{0,1:T(8,128)} fusion(bf16[2048,768]{1,0:T(8,128)(2,1)S(1)} %copy-done, f32[2048,768]{0,1:T(8,128)S(1)} %copy-done.5, f32[2048,768]{0,1:T(8,128)S(1)} %get-tuple-element.17, f32[2048]{0:T(1024)S(1)} %get-tuple-element.12, f32[2048]{0:T(1024)S(1)} %get-tuple-element.11), kind=kOutput, calls=%fused_computation.15 | convolution fusion | flops 2423783424 | bytes 18104320 | tf_op jit(solution)/shard_map/dot_general | solution.py:60
  63.5 0.0 all-reduce.2.cloned.1.call-update
  63.5 0.0 reduce-scatter.2.cloned.1.call-start
  63.5 8.7 %multiply_convert_fusion.1 = bf16[1024,768]{1,0:T(8,128)(2,1)} fusion(bf16[2048,1024]{0,1:T(8,128)(2,1)} %copy-done.2, f32[2048,768]{0,1:T(8,128)} %get-tuple-element.14, f32[2048]{0:T(1024)S(1)} %fusion.13), kind=kOutput, calls=%fused_computation.14 | convolution fusion | flops 3225944064 | bytes 12066816 | tf_op jit(solution)/shard_map/dot_general | solution.py:49
  72.2 0.0 reduce-scatter.2.cloned.1.call-update
  72.3 0.6 log_subtract_fusion
  72.9 254.9 %all-reduce.2.cloned.1.call-done = f32[768,768]{0,1:T(8,128)} async-done(((f32[768,768]{0,1:T(8,128)}), f32[768,768]{0,1:T(8,128)}) %all-reduce.2.cloned.1.call-update) | async-done | bytes 2359312 | tf_op jit(solution)/shard_map/psum | solution.py:63
  327.8 3.0 copy.9
  330.8 0.0 copy-done.3
  330.8 1.0 fusion.12
  331.9 1.7 add_add_fusion.1
  (8 shorter events, 0.0 us)
Async XLA Ops:
  8.0 20.3 %copy-start = (bf16[2048,768]{1,0:T(8,128)(2,1)S(1)}, bf16[2048,768]{1,0:T(8,128)(2,1)}, u32[]{:S(2)}) copy-start(bf16[2048,768]{1,0:T(8,128)(2,1)} %param.5) | copy-start | bytes 9437188
  8.0 11.7 %copy-start.1 = (s32[1024]{0:T(1024)S(1)}, s32[1024]{0:T(1024)}, u32[]{:S(2)}) copy-start(s32[1024]{0:T(1024)} %param.8) | copy-start | bytes 12292
  11.5 28.8 %all-to-all-start = ((bf16[16,64,768]{2,1,0:T(8,128)(2,1)}), bf16[16,64,768]{2,1,0:T(8,128)(2,1)}, u32[]{:S(2)}, u32[]{:S(2)}) async-start(bf16[16,64,768]{2,1,0:T(8,128)(2,1)} %stack.2), calls=%async_computation | async-start | bytes 3145728 | tf_op jit(solution)/shard_map/all_to_all | solution.py:24
  19.0 308.8 %all-reduce.2.cloned.1.call-start = ((), (), s32[]{:S(2)}) async-start(), calls=%async_computation.3 | async-start | bytes 4718592 | tf_op jit(solution)/shard_map/psum | solution.py:63
  28.3 5.9 %copy-start.4 = (s32[2048]{0:T(1024)S(1)}, s32[2048]{0:T(1024)}, u32[]{:S(2)}) copy-start(s32[2048]{0:T(1024)} %param.9) | copy-start | bytes 24580
  48.5 3.9 %copy-start.5 = (f32[2048,768]{0,1:T(8,128)S(1)}, f32[2048,768]{0,1:T(8,128)}, u32[]{:S(2)}) copy-start(f32[2048,768]{0,1:T(8,128)} %get-tuple-element.14) | copy-start | bytes 18874372
  52.3 6.6 %copy-start.2 = (bf16[2048,1024]{0,1:T(8,128)(2,1)}, bf16[2048,1024]{0,1:T(8,128)(2,1)S(1)}, u32[]{:S(2)}) copy-start(bf16[2048,1024]{0,1:T(8,128)(2,1)S(1)} %subtract_convert_fusion) | copy-start | bytes 12582916
  63.5 267.3 %reduce-scatter.2.cloned.1.call-start = ((), (), s32[]{:S(2)}) async-start(), calls=%async_computation.2 | async-start | bytes 1671168 | tf_op jit(solution)/shard_map/reduce_scatter | solution.py:47
  72.2 258.6 %copy-start.3 = (bf16[64,768]{1,0:T(8,128)(2,1)S(1)}, bf16[64,768]{1,0:T(8,128)(2,1)}, u32[]{:S(2)}) copy-start(bf16[64,768]{1,0:T(8,128)(2,1)} %param.7) | copy-start | bytes 294916
Sparse Core Ops, SparseCore 0:
  63.6 264.1 all-reduce.1
Sparse Core Ops, SparseCore 1:
  72.4 77.1 reduce-scatter.1
